TPU v7x, 32 devices: a whole 2x2x4 slice. The times are simulated.
32 devices in a mesh: sample: 8 (over y, x, core), token: 4 (over z).
Axes of the slice: x: 2, y: 2, z: 4, core: 2. Of those that a mesh axis runs over, the one named last changes fastest.
Arguments:
- activations: bfloat16 [16, 416, 768], P('sample', 'token'), may hold values from -6 to 6
- single: bfloat16 [416, 384], P('token'), may hold values from -6 to 6
- noise_index: int32 [16], P('sample'), may hold values from 0 to 199
- token_mask: int32 [416], replicated, may hold values 0 or 1
- pair_bias: bfloat16 [416, 16, 416], P('token', None, 'sample'), may hold values from -36 to 400
- fourier_freq: float32 [256], replicated, may hold values from -5 to 5
- fourier_phase: float32 [256], replicated, may hold values from 0 to 1
- noise_weight: bfloat16 [256, 384], replicated, may hold values from -0.375 to 0.375
- ada_weight: bfloat16 [384, 2304], replicated, may hold values from -0.3125 to 0.3125
- qkvg_weight: bfloat16 [768, 3072], P(None, 'sample'), may hold values from -0.21875 to 0.21875
- out_weight: bfloat16 [768, 768], P(None, 'sample'), may hold values from -0.21875 to 0.21875
Outputs:
- updated: bfloat16 [16, 416, 768], P('sample', 'token')
All inputs are finite; a program needn't handle non-finite values.
Results may differ from a plain program's by a relative error of at most 0.008.
Values may be sent and summed in bfloat16 or wider, within the bound.
No kernel may reach another device: no remote copies, remote signals or barrier semaphores. Data moves between devices by JAX's collectives and lax.ppermute only.
A program may use at most 128 MiB of HBM per device.

v0:
```python
import math
import jax
import jax.numpy as jnp
from jax import lax
from jax.sharding import PartitionSpec as P

HEADS = 16
STEPS = 200
sigma_data = 16.0
sigma_top = 160.0
sigma_low = 0.0004
exponent = 7.0
mask_penalty = 1000000000.0
norm_eps = 1e-05


def layer_norm(values):
    center = jnp.mean(values, axis=-1, keepdims=True)
    deviation = values - center
    spread = jnp.mean(deviation * deviation, axis=-1, keepdims=True)
    return deviation * lax.rsqrt(spread + norm_eps)


def noise_embedding(noise_index, fourier_freq, fourier_phase, noise_weight):
    fraction = noise_index.astype(jnp.float32) / (STEPS - 1)
    top_root = sigma_top ** (1.0 / exponent)
    low_root = sigma_low ** (1.0 / exponent)
    level_base = top_root + fraction * (low_root - top_root)
    sigma_level = sigma_data * level_base**exponent
    log_level = 0.25 * jnp.log(sigma_level / sigma_data)
    angles = 2.0 * math.pi * (log_level[:, None] * fourier_freq[None, :] + fourier_phase[None, :])
    features = layer_norm(jnp.cos(angles)).astype(jnp.bfloat16)
    return jnp.dot(features, noise_weight, preferred_element_type=jnp.float32)


def body(
    activations,
    single,
    noise_index,
    token_mask,
    pair_bias,
    fourier_freq,
    fourier_phase,
    noise_weight,
    ada_weight,
    qkvg_weight,
    out_weight,
):
    samples, query_count, model_width = activations.shape
    head_size = model_width // HEADS
    inverse = 1.0 / math.sqrt(head_size)
    penalty = (token_mask.astype(jnp.float32) - 1.0) * mask_penalty
    embedded = noise_embedding(noise_index, fourier_freq, fourier_phase, noise_weight)
    condition = layer_norm(single.astype(jnp.float32)[None, :, :] + embedded[:, None, :]).astype(
        jnp.bfloat16
    )
    modulate = jnp.dot(
        condition.reshape(samples * query_count, -1), ada_weight, preferred_element_type=jnp.float32
    )
    scale_part = modulate[:, :model_width]
    shift_part = modulate[:, model_width : 2 * model_width]
    out_gate = modulate[:, 2 * model_width :]
    flat_in = activations.reshape(samples * query_count, model_width).astype(jnp.float32)
    normed = (jax.nn.sigmoid(scale_part) * layer_norm(flat_in) + shift_part).astype(jnp.bfloat16)
    projected = jnp.dot(
        normed,
        lax.all_gather(qkvg_weight, "sample", axis=1, tiled=True),
        preferred_element_type=jnp.float32,
    ).astype(jnp.bfloat16)
    query_part = projected[:, :model_width]
    gate_part = projected[:, 3 * model_width :]
    travelling = projected[:, model_width : 3 * model_width].reshape(
        samples, query_count, 2 * model_width
    )
    query_heads = query_part.reshape(samples, query_count, HEADS, head_size)
    bias_rows = lax.all_gather(pair_bias, "sample", axis=2, tiled=True)
    top_old = jnp.full((samples, query_count, HEADS), -1e30, jnp.float32)
    segment = lax.all_gather(travelling, "token", axis=1, tiled=True)
    split_pairs = segment.reshape(samples, segment.shape[1], 2, HEADS, head_size)
    key_heads = split_pairs[:, :, 0]
    value_heads = split_pairs[:, :, 1]
    bias_block = bias_rows.astype(jnp.float32)
    scores = (
        jnp.einsum("sqhe,skhe->sqhk", query_heads, key_heads, preferred_element_type=jnp.float32)
        * inverse
    )
    scores = scores + bias_block[None] + penalty
    top_new = jnp.maximum(top_old, jnp.max(scores, axis=-1))
    weights = jnp.exp(scores - top_new[..., None])
    total_new = jnp.sum(weights, axis=-1)
    sum_new = jnp.einsum(
        "sqhk,skhe->sqhe",
        weights.astype(jnp.bfloat16),
        value_heads,
        preferred_element_type=jnp.float32,
    )
    result = (top_new, total_new, sum_new)
    top_last, total_last, sum_last = result
    attended = (sum_last / total_last[..., None]).reshape(samples * query_count, model_width)
    gated_rows = (attended * jax.nn.sigmoid(gate_part.astype(jnp.float32))).astype(jnp.bfloat16)
    output = (
        jax.nn.sigmoid(out_gate)
        * jnp.dot(
            gated_rows,
            lax.all_gather(out_weight, "sample", axis=1, tiled=True),
            preferred_element_type=jnp.float32,
        )
    ).astype(jnp.bfloat16)
    return output.reshape(samples, query_count, model_width)


def solution(mesh):
    placed = (
        P("sample", "token", None),
        P("token", None),
        P("sample"),
        P(),
        P("token", None, "sample"),
        P(),
        P(),
        P(),
        P(),
        P(None, "sample"),
        P(None, "sample"),
    )
    return jax.shard_map(
        body, mesh=mesh, in_specs=placed, out_specs=P("sample", "token", None), check_vma=False
    )
```

profile of v0, /device:TPU:0, one launch (start us, length us, event | category | flops | bytes accessed | tf_op | source)
XLA Modules:
  0.0 169.0 jit_solution(5035369524353801720)
XLA Ops:
  6.5 0.7 all-gather.5.cloned.1.call-update
  7.3 0.7 all-gather.9.cloned.1.call-update
  8.7 0.9 fusion.32
  9.7 0.9 multiply_reduce_fusion.2
  10.6 0.9 convert_element_type.47
  11.5 1.2 fusion.28
  13.2 1.1 convert_reduce_fusion
  14.4 1.2 multiply_reduce_fusion
  16.5 1.3 copy-done.3
  18.1 33.6 %all-gather.5.cloned.1.call-done = bf16[768,3072]{1,0:T(8,128)(2,1)} async-done(((bf16[768,384]{1,0:T(8,128)(2,1)}), bf16[768,3072]{1,0:T(8,128)(2,1)}) %all-gather.5.cloned.1.call-update) | async-done | bytes 4718608 | tf_op jit(solution)/shard_map/all_gather | solution.py:67
  51.7 3.5 %convolution_convert_fusion = bf16[208,3072]{1,0:T(8,128)(2,1)S(1)} fusion(bf16[208,768]{1,0:T(8,128)(2,1)S(1)} %fusion.15, bf16[768,3072]{1,0:T(8,128)(2,1)} %all-gather.5.cloned.1.call-done), kind=kOutput, calls=%fused_computation.6 | convolution fusion | flops 982106112 | bytes 6316032 | tf_op jit(solution)/shard_map/dot_general | solution.py:65
  55.2 1.3 copy.35
  57.2 22.5 %all-gather.9.cloned.1.call-done = bf16[104,16,416]{0,1,2:T(8,128)(2,1)} async-done(((bf16[104,16,52]{0,1,2:T(8,128)(2,1)}), bf16[104,16,416]{0,1,2:T(8,128)(2,1)}) %all-gather.9.cloned.1.call-update) | async-done | bytes 1384464 | tf_op jit(solution)/shard_map/all_gather | solution.py:76
  79.7 3.6 %copy.41 = f32[104,16,416]{0,2,1:T(8,128)} copy(bf16[104,16,416]{0,1,2:T(8,128)(2,1)} %all-gather.9.cloned.1.call-done) | data formatting | bytes 4153344 | tf_op jit(solution)/shard_map/convert_element_type | solution.py:82
  83.3 1.0 reshape.108
  84.3 50.7 %all-gather.7.cloned.1.call-done = bf16[2,416,1536]{2,0,1:T(2,128)(2,1)} async-done(((bf16[2,104,1536]{2,0,1:T(2,128)(2,1)}), bf16[2,416,1536]{2,0,1:T(2,128)(2,1)}) %all-gather.7.cloned.1.call-update) | async-done | bytes 2555920 | tf_op jit(solution)/shard_map/all_gather | solution.py:78
  135.0 8.5 %copy.36 = bf16[2,416,1536]{1,2,0:T(8,128)(2,1)} copy(bf16[2,416,1536]{2,0,1:T(2,128)(2,1)} %all-gather.7.cloned.1.call-done) | data formatting | bytes 5111808 | tf_op jit(solution)/shard_map/all_gather | solution.py:78
  143.5 4.8 %fusion.3 = (f32[2,104,16]{1,2,0:T(8,128)S(1)}, f32[2,16,416,104]{3,2,1,0:T(8,128)S(1)}) fusion(f32[416]{0:T(512)S(1)} %add_multiply_fusion, f32[104,16,416]{0,2,1:T(8,128)} %copy.41, bf16[2,104,16,48]{3,2,1,0:T(8,128)(2,1)S(1)} %reshape.108, bf16[2,416,2,16,48]{1,4,3,2,0:T(8,128)(2,1)} %bitcast.58), kind=kOutput, calls=%fused_computation.5 | convolution fusion | flops 138441472 | bytes 10852992 | tf_op jit(solution)/shard_map/sqhe,skhe->sqhk/dot_general | solution.py:84
  148.3 2.2 %fusion.1 = f32[2,104,16]{1,2,0:T(8,128)S(1)} fusion(f32[2,16,416,104]{3,2,1,0:T(8,128)S(1)} %get-tuple-element.8, f32[2,104,16]{1,2,0:T(8,128)S(1)} %broadcast_maximum_fusion, f32[416]{0:T(512)S(1)} %add_multiply_fusion, f32[104,16,416]{0,2,1:T(8,128)S(1)} %copy-done.1), kind=kLoop, calls=%fused_computation.3 | loop fusion | flops 6918912 | bytes 8334976 | tf_op jit(solution)/shard_map/reduce_sum | solution.py:90
  150.5 3.1 %fusion.11 = f32[2,104,16,48]{1,3,2,0:T(8,128)} fusion(f32[2,16,416,104]{3,2,1,0:T(8,128)S(1)} %get-tuple-element.8, f32[2,104,16]{1,2,0:T(8,128)S(1)} %broadcast_maximum_fusion, f32[416]{0:T(512)S(1)} %add_multiply_fusion, f32[104,16,416]{0,2,1:T(8,128)S(1)} %copy-done.1, bf16[2,416,2,16,48]{1,4,3,2,0:T(8,128)(2,1)S(1)} %bitcast.59, ...), kind=kOutput, calls=%fused_computation.14 | convolution fusion | flops 139988992 | bytes 12470272 | tf_op jit(solution)/shard_map/sqhk,skhe->sqhe/dot_general | solution.py:91
  153.6 1.9 %copy.48 = f32[2,104,16,48]{3,2,1,0:T(8,128)S(1)} copy(f32[2,104,16,48]{1,3,2,0:T(8,128)} %fusion.11) | data formatting | bytes 1277952 | tf_op jit(solution)/shard_map/reshape | solution.py:99
  155.5 1.5 reshape.109
  157.1 2.4 %all-gather.11.cloned.1.call-done = bf16[768,768]{0,1:T(8,128)(2,1)} async-done(((bf16[768,96]{0,1:T(8,128)(2,1)}), bf16[768,768]{0,1:T(8,128)(2,1)}) %all-gather.11.cloned.1.call-update) | async-done | bytes 1179664 | tf_op jit(solution)/shard_map/all_gather | solution.py:105
  159.4 3.0 %fusion.10 = bf16[208,768]{1,0:T(8,128)(2,1)} fusion(bf16[768,768]{0,1:T(8,128)(2,1)} %all-gather.11.cloned.1.call-done, f32[208,2304]{1,0:T(8,128)} %copy-done.3, f32[208,768]{1,0:T(8,128)} %reshape.109, bf16[208,3072]{1,0:T(8,128)(2,1)} %copy-done.4), kind=kOutput, calls=%fused_computation.13 | convolution fusion | flops 247123968 | bytes 3096576 | tf_op jit(solution)/shard_map/dot_general | solution.py:103
  (39 shorter events, 3.2 us)
Async XLA Ops:
  6.5 9.3 %copy-start = (bf16[384,2304]{1,0:T(8,128)(2,1)S(1)}, bf16[384,2304]{1,0:T(8,128)(2,1)}, u32[]{:S(2)}) copy-start(bf16[384,2304]{1,0:T(8,128)(2,1)} %param.19) | copy-start | bytes 5308420
  6.5 11.3 %copy-start.5 = (bf16[2,104,768]{2,1,0:T(8,128)(2,1)S(1)}, bf16[2,104,768]{2,1,0:T(8,128)(2,1)}, u32[]{:S(2)}) copy-start(bf16[2,104,768]{2,1,0:T(8,128)(2,1)} %param.11) | copy-start | bytes 958468
  6.5 45.1 %all-gather.5.cloned.1.call-start = ((), (), s32[]{:S(2)}) async-start(), calls=%async_computation | async-start | bytes 5308416 | tf_op jit(solution)/shard_map/all_gather | solution.py:67
  7.3 72.4 %all-gather.9.cloned.1.call-start = ((), (), s32[]{:S(2)}) async-start(), calls=%async_computation.2 | async-start | bytes 1916928 | tf_op jit(solution)/shard_map/all_gather | solution.py:76
  8.0 127.0 %all-gather.7.cloned.1.call-start = ((), (), s32[]{:S(2)}) async-start(), calls=%async_computation.1 | async-start | bytes 3194880 | tf_op jit(solution)/shard_map/all_gather | solution.py:78
  16.5 1.3 copy-start.3
  18.1 39.1 %copy-start.6 = (s32[416]{0:T(512)S(1)}, s32[416]{0:T(512)}, u32[]{:S(2)}) copy-start(s32[416]{0:T(512)} %param.14) | copy-start | bytes 4996
  55.2 28.1 %copy-start.4 = (bf16[208,3072]{1,0:T(8,128)(2,1)}, bf16[208,3072]{1,0:T(8,128)(2,1)S(1)}, u32[]{:S(2)}) copy-start(bf16[208,3072]{1,0:T(8,128)(2,1)S(1)} %convolution_convert_fusion) | copy-start | bytes 3833860
  56.6 102.9 %all-gather.11.cloned.1.call-start = ((), (), s32[]{:S(2)}) async-start(), calls=%async_computation.3 | async-start | bytes 1327104 | tf_op jit(solution)/shard_map/all_gather | solution.py:105
  143.5 4.8 %copy-start.1 = (f32[104,16,416]{0,2,1:T(8,128)S(1)}, f32[104,16,416]{0,2,1:T(8,128)}, u32[]{:S(2)}) copy-start(f32[104,16,416]{0,2,1:T(8,128)} %copy.41) | copy-start | bytes 8306692
  148.3 2.2 %copy-start.2 = (bf16[2,416,1536]{1,2,0:T(8,128)(2,1)S(1)}, bf16[2,416,1536]{1,2,0:T(8,128)(2,1)}, u32[]{:S(2)}) copy-start(bf16[2,416,1536]{1,2,0:T(8,128)(2,1)} %copy.36) | copy-start | bytes 7667716
Sparse Core Ops, SparseCore 0:
  9.2 42.4 all-gather.4
  53.5 26.1 all-gather.8
  81.3 53.6 all-gather.6
  136.7 22.6 all-gather.10
where the time goes:
time: 170 us; the launch traced here: 169 us
  waiting for transfers between devices  111 us (65%)
  local copies, waits for them, and re-layouts  19.6 us (12%)
  matrix products  16.3 us (10%)
  between operations  13.3 us (8%)
  other arithmetic  8.68 us (5%)
    all_gather x1, waiting for transfers between devices, body(): segment = lax.all_gather(travelling, 'token', axis=1, tiled=True)  50.7 us
    all_gather x1, waiting for transfers between devices, body(): lax.all_gather(qkvg_weight, 'sample', axis=1, tiled=True)  33.6 us
    all_gather x1, waiting for transfers between devices, body(): bias_rows = lax.all_gather(pair_bias, 'sample', axis=2, tiled=True)  22.5 us
    all_gather x1, local copies, waits for them, and re-layouts, body(): segment = lax.all_gather(travelling, 'token', axis=1, tiled=True)  8.52 us
    dot_general x1, matrix products, body(): jnp.einsum('sqhe,skhe->sqhk', query_heads, key_heads, preferred_element_t...  4.79 us
    convert_element_type x1, local copies, waits for them, and re-layouts, body(): bias_block = bias_rows.astype(jnp.float32)  3.56 us
    dot_general x1, matrix products, body(): jnp.dot(normed, lax.all_gather(qkvg_weight, 'sample', axis=1, tiled=True)...  3.51 us
    reshape x2, local copies, waits for them, and re-layouts, body(): (sum_last / total_last[..., None]).reshape(samples * query_count, model_w...  3.45 us
  transfers between devices with their start and end apart: 4, of which 4 were waited for; matrix products, arithmetic and copies ran while one was open for 24% of the time, Pallas kernels for 0%

commit v1 on v0

--- a/solution.py
+++ b/solution.py
@@ -75,7 +75,14 @@
     query_heads = query_part.reshape(samples, query_count, HEADS, head_size)
     bias_rows = lax.all_gather(pair_bias, "sample", axis=2, tiled=True)
     top_old = jnp.full((samples, query_count, HEADS), -1e30, jnp.float32)
-    segment = lax.all_gather(travelling, "token", axis=1, tiled=True)
+    ring = [travelling]
+    for hop in range(3):
+        ring.append(lax.ppermute(ring[-1], "token", [(dev, (dev + 1) % 4) for dev in range(4)]))
+    segment = jnp.roll(
+        jnp.concatenate(ring[::-1], axis=1),
+        (lax.axis_index("token") + 1) * ring[0].shape[1],
+        axis=1,
+    )
     split_pairs = segment.reshape(samples, segment.shape[1], 2, HEADS, head_size)
     key_heads = split_pairs[:, :, 0]
     value_heads = split_pairs[:, :, 1]

time: 170 us -> 148 us (0.87)
  waiting for transfers between devices: 111 us -> 75.2 us
  local copies, waits for them, and re-layouts: 19.6 us -> 31.8 us
    all_gather x1 -> x0, waiting for transfers between devices: 50.7 us -> none  [body(): segment = lax.all_gather(travelling, 'token', axis=1, tiled=True)]
    ppermute x0 -> x3, waiting for transfers between devices: none -> 41.5 us  [body(): lax.ppermute(ring[-1], 'token', [(dev, (dev + 1) % 4) for dev in range(4)])]
    all_gather x1, waiting for transfers between devices: 22.5 us -> 0.02 us  [body(): bias_rows = lax.all_gather(pair_bias, 'sample', axis=2, tiled=True)]
    concatenate x0 -> x1, local copies, waits for them, and re-layouts: none -> 9.86 us  [body(): jnp.roll(jnp.concatenate(ring[::-1], axis=1), (lax.axis_index('token') +...]
    all_gather x1 -> x0, local copies, waits for them, and re-layouts: 8.52 us -> none  [body(): segment = lax.all_gather(travelling, 'token', axis=1, tiled=True)]
    ppermute x0 -> x3, local copies, waits for them, and re-layouts: none -> 6.07 us  [body(): lax.ppermute(ring[-1], 'token', [(dev, (dev + 1) % 4) for dev in range(4)])]
    dynamic_slice x0 -> x1, local copies, waits for them, and re-layouts: none -> 4.01 us  [body(): jnp.roll(jnp.concatenate(ring[::-1], axis=1), (lax.axis_index('token') +...]
    dot_general x1, matrix products: 4.79 us -> 2.29 us  [body(): jnp.einsum('sqhe,skhe->sqhk', query_heads, key_heads, preferred_element_t...]
  transfers between devices with their start and end apart: 4 -> 6, of which waited for: 4 -> 4; matrix products, arithmetic and copies ran while one was open for 24% -> 35% of each run, Pallas kernels for 0% -> 0%
where the time goes in v1:
time: 148 us; the launch traced here: 147 us
  waiting for transfers between devices  75.2 us (51%)
  local copies, waits for them, and re-layouts  31.8 us (21%)
  matrix products  15.2 us (10%)
  between operations  13.3 us (9%)
  other arithmetic  10 us (7%)
  starting transfers between devices  1.63 us (1%)
    ppermute x3, waiting for transfers between devices, body(): lax.ppermute(ring[-1], 'token', [(dev, (dev + 1) % 4) for dev in range(4)])  41.5 us
    all_gather x1, waiting for transfers between devices, body(): lax.all_gather(qkvg_weight, 'sample', axis=1, tiled=True)  32.2 us
    concatenate x1, local copies, waits for them, and re-layouts, body(): jnp.roll(jnp.concatenate(ring[::-1], axis=1), (lax.axis_index('token') +...  9.86 us
    ppermute x3, local copies, waits for them, and re-layouts, body(): lax.ppermute(ring[-1], 'token', [(dev, (dev + 1) % 4) for dev in range(4)])  6.07 us
    dynamic_slice x1, local copies, waits for them, and re-layouts, body(): jnp.roll(jnp.concatenate(ring[::-1], axis=1), (lax.axis_index('token') +...  4.01 us
    convert_element_type x1, local copies, waits for them, and re-layouts, body(): bias_block = bias_rows.astype(jnp.float32)  3.66 us
    dot_general x1, matrix products, body(): jnp.dot(normed, lax.all_gather(qkvg_weight, 'sample', axis=1, tiled=True)...  3.56 us
    reshape x2, local copies, waits for them, and re-layouts, body(): (sum_last / total_last[..., None]).reshape(samples * query_count, model_w...  3.47 us
  transfers between devices with their start and end apart: 6, of which 4 were waited for; matrix products, arithmetic and copies ran while one was open for 35% of the time, Pallas kernels for 0%

profile of v1, /device:TPU:0, one launch (start us, length us, event | category | flops | bytes accessed | tf_op | source)
XLA Modules:
  0.0 147.1 jit_solution(17086643163549742535)
XLA Ops:
  11.5 1.2 fusion.28
  14.3 1.2 multiply_reduce_fusion
  15.7 2.0 %fusion.33 = f32[208,2304]{1,0:T(8,128)} fusion(bf16[208,384]{1,0:T(8,128)(2,1)S(1)} %fusion.26, bf16[384,2304]{1,0:T(8,128)(2,1)S(1)} %copy-done), kind=kOutput, calls=%fused_computation.58 | convolution fusion | flops 368050176 | bytes 3846144 | tf_op jit(solution)/shard_map/dot_general | solution.py:57
  17.8 1.7 %fusion.15 = bf16[208,768]{1,0:T(8,128)(2,1)S(1)} fusion(f32[208,2304]{1,0:T(8,128)} %fusion.33, bf16[2,104,768]{2,1,0:T(8,128)(2,1)S(1)} %copy-done.4, f32[208]{0:T(256)S(1)} %rsqrt.34, f32[208]{0:T(256)S(1)} %div.49), kind=kLoop, calls=%fused_computation.17 | loop fusion | flops 1437696 | bytes 1918592 | tf_op jit(solution)/shard_map/convert_element_type | solution.py:64
  19.5 32.2 %all-gather.4.cloned.1.call-done = bf16[768,3072]{1,0:T(8,128)(2,1)} async-done(((bf16[768,384]{1,0:T(8,128)(2,1)}), bf16[768,3072]{1,0:T(8,128)(2,1)}) %all-gather.4.cloned.1.call-update) | async-done | bytes 4718608 | tf_op jit(solution)/shard_map/all_gather | solution.py:67
  51.7 3.6 %convolution_convert_fusion = bf16[208,3072]{1,0:T(8,128)(2,1)S(1)} fusion(bf16[208,768]{1,0:T(8,128)(2,1)S(1)} %fusion.15, bf16[768,3072]{1,0:T(8,128)(2,1)} %all-gather.4.cloned.1.call-done), kind=kOutput, calls=%fused_computation.6 | convolution fusion | flops 982106112 | bytes 6316032 | tf_op jit(solution)/shard_map/dot_general | solution.py:65
  55.2 1.1 copy-done.2
  56.4 1.5 %collective-permute-start = (bf16[2,104,1536]{2,1,0:T(8,128)(2,1)S(1)}, bf16[2,104,1536]{2,1,0:T(8,128)(2,1)S(1)}, u32[]{:S(2)}, u32[]{:S(2)}) collective-permute-start(bf16[2,104,1536]{2,1,0:T(8,128)(2,1)S(1)} %bitcast.60), channel_id=1, source_target_pairs={{0,1},{1,2},{2,3},{3,0},{4,5},{5,6},{6,7},{7,4},{8,9},{9,10},{10,1... | collective-permute-start | bytes 1916936 | tf_op jit(solution)/shard_map/ppermute | solution.py:80
  58.0 16.8 %collective-permute-done = bf16[2,104,1536]{2,1,0:T(8,128)(2,1)S(1)} collective-permute-done((bf16[2,104,1536]{2,1,0:T(8,128)(2,1)S(1)}, bf16[2,104,1536]{2,1,0:T(8,128)(2,1)S(1)}, u32[]{:S(2)}, u32[]{:S(2)}) %collective-permute-start) | collective-permute-done | bytes 639008 | tf_op jit(solution)/shard_map/ppermute | solution.py:80
  75.7 17.6 %collective-permute-done.1 = bf16[2,104,1536]{2,1,0:T(8,128)(2,1)} collective-permute-done((bf16[2,104,1536]{2,1,0:T(8,128)(2,1)S(1)}, bf16[2,104,1536]{2,1,0:T(8,128)(2,1)}, u32[]{:S(2)}, u32[]{:S(2)}) %collective-permute-start.1) | collective-permute-done | bytes 639008 | tf_op jit(solution)/shard_map/ppermute | solution.py:80
  93.4 3.7 %copy.55 = f32[104,16,416]{0,2,1:T(8,128)} copy(bf16[104,16,416]{0,1,2:T(8,128)(2,1)} %all-gather.6.cloned.1.call-done) | data formatting | bytes 4153344 | tf_op jit(solution)/shard_map/convert_element_type | solution.py:89
  97.4 1.9 %reshape.108 = bf16[2,104,16,48]{3,2,1,0:T(8,128)(2,1)} reshape(bf16[208,768]{1,0:T(8,128)(2,1)S(1)} %slice-done) | data formatting | bytes 638976 | tf_op jit(solution)/shard_map/reshape | solution.py:75
  99.4 1.5 copy.45
  100.8 2.3 %copy.44 = bf16[2,104,1536]{1,2,0:T(8,128)(2,1)} copy(bf16[2,104,1536]{2,1,0:T(8,128)(2,1)} %collective-permute-done.1) | data formatting | bytes 1277952 | tf_op jit(solution)/shard_map/ppermute | solution.py:80
  103.1 7.1 %collective-permute-done.2 = bf16[2,104,1536]{2,1,0:T(8,128)(2,1)} collective-permute-done((bf16[2,104,1536]{2,1,0:T(8,128)(2,1)}, bf16[2,104,1536]{2,1,0:T(8,128)(2,1)}, u32[]{:S(2)}, u32[]{:S(2)}) %collective-permute-start.2) | collective-permute-done | bytes 639008 | tf_op jit(solution)/shard_map/ppermute | solution.py:80
  110.2 2.3 %copy.43 = bf16[2,104,1536]{1,2,0:T(8,128)(2,1)} copy(bf16[2,104,1536]{2,1,0:T(8,128)(2,1)} %collective-permute-done.2) | data formatting | bytes 1277952 | tf_op jit(solution)/shard_map/ppermute | solution.py:80
  112.5 9.9 %concatenate.6 = bf16[2,832,1536]{1,2,0:T(8,128)(2,1)} concatenate(bf16[2,104,1536]{1,2,0:T(8,128)(2,1)} %copy.43, bf16[2,104,1536]{1,2,0:T(8,128)(2,1)} %copy.44, bf16[2,104,1536]{1,2,0:T(8,128)(2,1)S(1)} %copy.45, bf16[2,104,1536]{1,2,0:T(8,128)(2,1)S(1)} %copy.46, bf16[2,104,1536]{1,2,0:T(8,128)(2,1)} %copy.43, bf16[2,104,1536]{1,2,0:T(8,128)(2,1)} %copy.44, ...), dimensions={1} | concatenate | bytes 10223616 | tf_op jit(solution)/shard_map/jit(_roll_dynamic)/concatenate | solution.py:81
  122.4 4.0 %constant_dynamic-slice_fusion = bf16[2,416,1536]{1,2,0:T(8,128)(2,1)S(1)} fusion(bf16[2,832,1536]{1,2,0:T(8,128)(2,1)} %concatenate.6, s32[]{:T(128)S(6)} %select_n.14), kind=kLoop, calls=%fused_computation.53 | loop fusion | bytes 5111812 | tf_op jit(solution)/shard_map/jit(_roll_dynamic)/dynamic_slice | solution.py:81
  126.4 2.3 %fusion.3 = (f32[2,104,16]{1,2,0:T(8,128)S(1)}, f32[2,16,416,104]{3,2,1,0:T(8,128)S(1)}) fusion(f32[416]{0:T(512)S(1)} %add_multiply_fusion, f32[104,16,416]{0,2,1:T(8,128)S(1)} %copy-done.1, bf16[2,104,16,48]{3,2,1,0:T(8,128)(2,1)S(1)} %copy-done.3, bf16[2,416,2,16,48]{1,4,3,2,0:T(8,128)(2,1)S(1)} %bitcast.58), kind=kOutput, calls=%fused_computation.5 | convolution fusion | flops 138441472 | bytes 11385856 | tf_op jit(solution)/shard_map/sqhe,skhe->sqhk/dot_general | solution.py:91
  128.8 2.2 %fusion.1 = f32[2,104,16]{1,2,0:T(8,128)S(1)} fusion(f32[2,16,416,104]{3,2,1,0:T(8,128)S(1)} %get-tuple-element.8, f32[2,104,16]{1,2,0:T(8,128)S(1)} %broadcast_maximum_fusion, f32[416]{0:T(512)S(1)} %add_multiply_fusion, f32[104,16,416]{0,2,1:T(8,128)S(1)} %copy-done.1), kind=kLoop, calls=%fused_computation.3 | loop fusion | flops 6918912 | bytes 8334976 | tf_op jit(solution)/shard_map/reduce_sum | solution.py:97
  130.9 3.1 %fusion.11 = f32[2,104,16,48]{1,3,2,0:T(8,128)} fusion(f32[2,16,416,104]{3,2,1,0:T(8,128)S(1)} %get-tuple-element.8, f32[2,104,16]{1,2,0:T(8,128)S(1)} %broadcast_maximum_fusion, f32[416]{0:T(512)S(1)} %add_multiply_fusion, f32[104,16,416]{0,2,1:T(8,128)S(1)} %copy-done.1, bf16[2,416,2,16,48]{1,4,3,2,0:T(8,128)(2,1)S(1)} %bitcast.59, ...), kind=kOutput, calls=%fused_computation.14 | convolution fusion | flops 139988992 | bytes 12470272 | tf_op jit(solution)/shard_map/sqhk,skhe->sqhe/dot_general | solution.py:98
  134.1 1.9 %copy.62 = f32[2,104,16,48]{3,2,1,0:T(8,128)S(1)} copy(f32[2,104,16,48]{1,3,2,0:T(8,128)} %fusion.11) | data formatting | bytes 1277952 | tf_op jit(solution)/shard_map/reshape | solution.py:106
  136.0 1.6 %reshape.109 = f32[208,768]{1,0:T(8,128)} reshape(f32[2,104,16,48]{3,2,1,0:T(8,128)S(1)} %copy.62) | data formatting | bytes 1277952 | tf_op jit(solution)/shard_map/reshape | solution.py:106
  137.5 3.0 %fusion.10 = bf16[208,768]{1,0:T(8,128)(2,1)} fusion(bf16[768,768]{0,1:T(8,128)(2,1)} %all-gather.8.cloned.1.call-done, f32[208,2304]{1,0:T(8,128)} %fusion.33, f32[208,768]{1,0:T(8,128)} %reshape.109, bf16[208,3072]{1,0:T(8,128)(2,1)} %copy-done.2), kind=kOutput, calls=%fused_computation.13 | convolution fusion | flops 247123968 | bytes 3096576 | tf_op jit(solution)/shard_map/dot_general | solution.py:110
  (47 shorter events, 8.2 us)
Async XLA Ops:
  6.5 9.1 %copy-start = (bf16[384,2304]{1,0:T(8,128)(2,1)S(1)}, bf16[384,2304]{1,0:T(8,128)(2,1)}, u32[]{:S(2)}) copy-start(bf16[384,2304]{1,0:T(8,128)(2,1)} %param.19) | copy-start | bytes 5308420
  6.5 11.3 %copy-start.4 = (bf16[2,104,768]{2,1,0:T(8,128)(2,1)S(1)}, bf16[2,104,768]{2,1,0:T(8,128)(2,1)}, u32[]{:S(2)}) copy-start(bf16[2,104,768]{2,1,0:T(8,128)(2,1)} %param.11) | copy-start | bytes 958468
  6.5 45.1 %all-gather.4.cloned.1.call-start = ((), (), s32[]{:S(2)}) async-start(), calls=%async_computation | async-start | bytes 5308416 | tf_op jit(solution)/shard_map/all_gather | solution.py:67
  7.3 86.1 %all-gather.6.cloned.1.call-start = ((), (), s32[]{:S(2)}) async-start(), calls=%async_computation.1 | async-start | bytes 1916928 | tf_op jit(solution)/shard_map/all_gather | solution.py:76
  8.0 129.5 %all-gather.8.cloned.1.call-start = ((), (), s32[]{:S(2)}) async-start(), calls=%async_computation.2 | async-start | bytes 1327104 | tf_op jit(solution)/shard_map/all_gather | solution.py:112
  19.5 73.9 %copy-start.6 = (s32[416]{0:T(512)S(1)}, s32[416]{0:T(512)}, u32[]{:S(2)}) copy-start(s32[416]{0:T(512)} %param.14) | copy-start | bytes 4996
  55.2 1.1 copy-start.2
  56.4 18.4 %collective-permute-start = (bf16[2,104,1536]{2,1,0:T(8,128)(2,1)S(1)}, bf16[2,104,1536]{2,1,0:T(8,128)(2,1)S(1)}, u32[]{:S(2)}, u32[]{:S(2)}) collective-permute-start(bf16[2,104,1536]{2,1,0:T(8,128)(2,1)S(1)} %bitcast.60), channel_id=1, source_target_pairs={{0,1},{1,2},{2,3},{3,0},{4,5},{5,6},{6,7},{7,4},{8,9},{9,10},{10,1... | collective-permute-start | bytes 1916936 | tf_op jit(solution)/shard_map/ppermute | solution.py:80
  74.8 0.9 copy-start.5
  75.7 17.6 %collective-permute-start.1 = (bf16[2,104,1536]{2,1,0:T(8,128)(2,1)S(1)}, bf16[2,104,1536]{2,1,0:T(8,128)(2,1)}, u32[]{:S(2)}, u32[]{:S(2)}) collective-permute-start(bf16[2,104,1536]{2,1,0:T(8,128)(2,1)S(1)} %collective-permute-done), channel_id=1, source_target_pairs={{0,1},{1,2},{2,3},{3,0},{4,5},{5,6},{6,7},{7,4},{8,9},{9,10},{10,1... | collective-permute-start | bytes 1916936 | tf_op jit(solution)/shard_map/ppermute | solution.py:80
  93.3 16.9 %collective-permute-start.2 = (bf16[2,104,1536]{2,1,0:T(8,128)(2,1)}, bf16[2,104,1536]{2,1,0:T(8,128)(2,1)}, u32[]{:S(2)}, u32[]{:S(2)}) collective-permute-start(bf16[2,104,1536]{2,1,0:T(8,128)(2,1)} %collective-permute-done.1), channel_id=1, source_target_pairs={{0,1},{1,2},{2,3},{3,0},{4,5},{5,6},{6,7},{7,4},{8,9},{9,10},{10,1... | collective-permute-start | bytes 1916936 | tf_op jit(solution)/shard_map/ppermute | solution.py:80
  93.3 4.1 %slice-start = ((bf16[208,3072]{1,0:T(8,128)(2,1)}), bf16[208,768]{1,0:T(8,128)(2,1)S(1)}, s32[]{:S(2)}) async-start(bf16[208,3072]{1,0:T(8,128)(2,1)} %copy-done.2), calls=%async_computation.3 | async-start | bytes 638976 | tf_op jit(solution)/shard_map/slice | solution.py:70
  122.4 4.0 %copy-start.1 = (f32[104,16,416]{0,2,1:T(8,128)S(1)}, f32[104,16,416]{0,2,1:T(8,128)}, u32[]{:S(2)}) copy-start(f32[104,16,416]{0,2,1:T(8,128)} %copy.55) | copy-start | bytes 8306692
  122.4 4.0 %copy-start.3 = (bf16[2,104,16,48]{3,2,1,0:T(8,128)(2,1)S(1)}, bf16[2,104,16,48]{3,2,1,0:T(8,128)(2,1)}, u32[]{:S(2)}) copy-start(bf16[2,104,16,48]{3,2,1,0:T(8,128)(2,1)} %reshape.108) | copy-start | bytes 958468
Sparse Core Ops, SparseCore 0:
  9.2 42.4 all-gather.3
  53.5 26.1 all-gather.5
  93.4 24.3 all-gather.7
